TPU v7x, 32 devices: a whole 2x2x4 slice. The times are simulated.
32 devices in a mesh: blk: 16 (over z, y, core), rep: 2 (over x).
Axes of the slice: x: 2, y: 2, z: 4, core: 2. Of those that a mesh axis runs over, the one named last changes fastest.
Arguments:
- grad_out: bfloat16 [24576, 256], P('blk'), may hold values from -6 to 6
- pre_act: bfloat16 [24576, 256], P('blk'), may hold values from -6 to 6
- prev_pre: bfloat16 [24576, 256], P(('blk', 'rep')), may hold values from -6 to 6
- weight: bfloat16 [256, 256], replicated, may hold values from -0.375 to 0.375
- block_values: bfloat16 [3840, 128, 128], P(('blk', 'rep')), may hold values from -0.25 to 0.25
- block_rows: int32 [3840], P(('blk', 'rep')), may hold values from 0 to 11, as said below
- block_cols: int32 [3840], P(('blk', 'rep')), may hold values from 0 to 59
Outputs:
- grad_in: bfloat16 [24576, 256], P(('blk', 'rep'))
- grad_weight: float32 [256, 256], replicated
Inputs may be any that keep to these rules, and one draw needn't show every extreme that they name: The blocks of the 2 devices of one stripe sit at distinct (block_rows, block_cols) positions.
All inputs are finite; a program needn't handle non-finite values.
Results may differ from a plain program's by a relative error of at most 0.0049.
Values sent between devices are 32-bit elements; how exact they have to be, the bound alone decides.
A program may use at most 192 MiB of HBM per device.

v0:
```python
import math

import jax
import jax.numpy as jnp
from jax import lax
from jax.sharding import PartitionSpec as P

HALO = 2


def shifted(value, axis, by):
    devices = lax.axis_size(axis)
    return lax.ppermute(value, axis, [(i, (i + by) % devices) for i in range(devices)])


def local(grad_out, pre_act, prev_pre, weight, block_values, block_rows, block_cols):
    stripe_rows, width = grad_out.shape
    block_size = block_values.shape[1]
    stripe_blocks = stripe_rows // block_size
    spans = 2 * HALO + 1
    masked = grad_out * (pre_act > 0).astype(jnp.bfloat16)
    picked = masked.reshape(stripe_blocks, block_size, width)[block_rows]
    tiles = jnp.einsum("kab,kaf->kbf", block_values, picked, preferred_element_type=jnp.float32)
    window = jax.ops.segment_sum(tiles, block_cols, num_segments=spans * stripe_blocks)
    window = window.reshape(spans, stripe_rows, width)
    total = window[HALO]
    for position in range(spans):
        if position != HALO:
            total = total + shifted(window[position], "blk", position - HALO)
    mine = lax.psum_scatter(total, "rep", scatter_dimension=0, tiled=True)
    dy_rows = mine.astype(jnp.bfloat16)
    feats = jnp.maximum(prev_pre, jnp.zeros_like(prev_pre))
    weight_term = jnp.dot(feats.T, dy_rows, preferred_element_type=jnp.float32)
    node_count = stripe_rows * lax.axis_size("blk")
    grad_weight = lax.psum(weight_term, ("blk", "rep")) * (1.0 / math.sqrt(node_count))
    grad_in = (
        jnp.dot(dy_rows, weight.T, preferred_element_type=jnp.float32)
        * (prev_pre > 0).astype(jnp.float32)
    ).astype(jnp.bfloat16)
    return (grad_in, grad_weight)


def solution(mesh):
    in_specs = (
        P("blk", None),
        P("blk", None),
        P(("blk", "rep"), None),
        P(),
        P(("blk", "rep"), None, None),
        P(("blk", "rep")),
        P(("blk", "rep")),
    )
    out_specs = (P(("blk", "rep"), None), P())
    return jax.shard_map(local, mesh=mesh, in_specs=in_specs, out_specs=out_specs, check_vma=False)
```

profile of v0, /device:TPU:0, one launch (start us, length us, event | category | flops | bytes accessed | tf_op | source)
XLA Modules:
  0.0 365.0 jit_solution(13241581030041668142)
XLA Ops:
  7.2 0.0 copy-start
  7.2 0.0 reduce-scatter.2.cloned.1.call-start
  7.2 0.7 compare_select_fusion.1
  7.9 1.5 compare_select_fusion
  9.4 6.4 %gather_fusion = bf16[120,128,256]{2,1,0:T(8,128)(2,1)} fusion(bf16[12,128,256]{2,1,0:T(8,128)(2,1)S(1)} %bitcast.18, s32[1024]{0:T(1024)S(1)} %pad_clamp_fusion), kind=kCustom, calls=%fused_computation | custom fusion | bytes 15729120 | tf_op jit(solution)/shard_map/gather | solution.py:22
  15.8 12.1 %convolution_bitcast_fusion = f32[120,128,256]{1,2,0:T(8,128)} fusion(bf16[120,128,256]{2,1,0:T(8,128)(2,1)} %gather_fusion, bf16[120,128,128]{2,1,0:T(8,128)(2,1)} %param.11), kind=kOutput, calls=%fused_computation.2 | convolution fusion | flops 1006632960 | bytes 27525120 | tf_op jit(solution)/shard_map/kab,kaf->kbf/dot_general | solution.py:23
  27.9 15.6 %copy.11 = f32[120,128,256]{2,1,0:T(8,128)} copy(f32[120,128,256]{1,2,0:T(8,128)} %convolution_bitcast_fusion) | data formatting | bytes 31457280 | tf_op jit(solution)/shard_map/kab,kaf->kbf/dot_general | solution.py:23
  43.5 0.0 copy-start.3
  43.5 4.1 %broadcast_in_dim.9 = f32[60,128,256]{2,1,0:T(8,128)} broadcast(f32[]{:T(128)} %constant.2.clone.1), dimensions={} | broadcast | bytes 7864324 | tf_op jit(solution)/shard_map/broadcast_in_dim | solution.py:24
  47.6 0.0 copy-done.3
  47.6 37.6 %scatter_fusion = f32[60,128,256]{2,1,0:T(8,128)} fusion(f32[60,128,256]{2,1,0:T(8,128)} %broadcast_in_dim.9, s32[120]{0:T(128)S(1)} %copy-done.3, f32[120,128,256]{2,1,0:T(8,128)} %copy.11), kind=kCustom, calls=%fused_computation.1 | custom fusion | flops 3932160 | bytes 47186400 | tf_op jit(solution)/shard_map/scatter-add | solution.py:24
  85.2 3.9 %fusion.10 = (f32[12,128,256]{2,1,0:T(8,128)S(1)}, f32[12,128,256]{2,1,0:T(8,128)S(1)}, f32[12,128,256]{2,1,0:T(8,128)S(1)}, f32[12,128,256]{2,1,0:T(8,128)S(1)}, f32[12,128,256]{2,1,0:T(8,128)S(1)}) fusion(f32[60,128,256]{2,1,0:T(8,128)} %scatter_fusion), kind=kLoop, calls=%fused_computation.19 | loop fusion | bytes 15728640 | tf_op jit(solution)/shard_map/slice | solution.py:26
  89.0 3.5 collective-permute-start.3
  92.5 0.0 collective-permute-start.2
  92.5 4.4 %collective-permute-start.1 = (f32[1536,256]{1,0:T(8,128)S(1)}, f32[1536,256]{1,0:T(8,128)S(1)}, u32[]{:S(2)}, u32[]{:S(2)}) collective-permute-start(f32[1536,256]{1,0:T(8,128)S(1)} %bitcast.20), channel_id=1, source_target_pairs={{0,30},{2,0},{4,2},{6,4},{8,6},{10,8},{12,10},{14,12},{16,14},{18,... | collective-permute-start | bytes 4718600 | tf_op jit(solution)/shard_map/ppermute | solution.py:13
  97.0 0.1 collective-permute-start
  97.0 80.8 %collective-permute-done.3 = f32[1536,256]{1,0:T(8,128)S(1)} collective-permute-done((f32[1536,256]{1,0:T(8,128)S(1)}, f32[1536,256]{1,0:T(8,128)S(1)}, u32[]{:S(2)}, u32[]{:S(2)}) %collective-permute-start.3) | collective-permute-done | bytes 1572896 | tf_op jit(solution)/shard_map/ppermute | solution.py:13
  177.9 0.0 collective-permute-done.2
  177.9 0.0 collective-permute-done.1
  177.9 19.3 %collective-permute-done = f32[1536,256]{1,0:T(8,128)S(1)} collective-permute-done((f32[1536,256]{1,0:T(8,128)S(1)}, f32[1536,256]{1,0:T(8,128)S(1)}, u32[]{:S(2)}, u32[]{:S(2)}) %collective-permute-start) | collective-permute-done | bytes 1572896 | tf_op jit(solution)/shard_map/ppermute | solution.py:13
  197.1 1.7 fusion.2
  198.8 0.0 copy-start.2
  198.8 0.0 reduce-scatter.2.cloned.1.call-update
  198.8 0.0 all-reduce.2.cloned.1.call-start
  198.9 24.9 %reduce-scatter.2.cloned.1.call-done = f32[768,256]{1,0:T(8,128)} async-done(((f32[1536,256]{1,0:T(8,128)}), f32[768,256]{1,0:T(8,128)}) %reduce-scatter.2.cloned.1.call-update) | async-done | bytes 786448 | tf_op jit(solution)/shard_map/reduce_scatter | solution.py:30
  223.8 0.0 copy-done.2
  223.8 0.0 copy-start.1
  223.8 2.2 fusion.4
  226.0 0.0 all-reduce.2.cloned.1.call-update
  226.0 0.0 copy-done
  226.1 0.0 copy-done.1
  226.1 1.0 fusion.3
  227.1 129.4 %all-reduce.2.cloned.1.call-done = f32[256,256]{1,0:T(8,128)} async-done(((f32[256,256]{1,0:T(8,128)}), f32[256,256]{1,0:T(8,128)}) %all-reduce.2.cloned.1.call-update) | async-done | bytes 262160 | tf_op jit(solution)/shard_map/psum | solution.py:35
  356.5 1.7 broadcast_multiply_fusion
  (1 shorter events, 0.0 us)
Async XLA Ops:
  7.2 218.9 %copy-start = (bf16[256,256]{1,0:T(8,128)(2,1)S(1)}, bf16[256,256]{1,0:T(8,128)(2,1)}, u32[]{:S(2)}) copy-start(bf16[256,256]{1,0:T(8,128)(2,1)} %param.10) | copy-start | bytes 393220
  7.2 216.6 %reduce-scatter.2.cloned.1.call-start = ((), (), s32[]{:S(2)}) async-start(), calls=%async_computation.1 | async-start | bytes 2359296 | tf_op jit(solution)/shard_map/reduce_scatter | solution.py:30
  43.5 4.1 %copy-start.3 = (s32[120]{0:T(128)S(1)}, s32[120]{0:T(128)}, u32[]{:S(2)}) copy-start(s32[120]{0:T(128)} %param.13) | copy-start | bytes 1444
  89.0 88.8 %collective-permute-start.3 = (f32[1536,256]{1,0:T(8,128)S(1)}, f32[1536,256]{1,0:T(8,128)S(1)}, u32[]{:S(2)}, u32[]{:S(2)}) collective-permute-start(f32[1536,256]{1,0:T(8,128)S(1)} %bitcast.22), channel_id=1, source_target_pairs={{0,4},{2,6},{4,8},{6,10},{8,12},{10,14},{12,16},{14,18},{16,20},{1... | collective-permute-start | bytes 4718600 | tf_op jit(solution)/shard_map/ppermute | solution.py:13
  92.5 85.3 %collective-permute-start.2 = (f32[1536,256]{1,0:T(8,128)S(1)}, f32[1536,256]{1,0:T(8,128)S(1)}, u32[]{:S(2)}, u32[]{:S(2)}) collective-permute-start(f32[1536,256]{1,0:T(8,128)S(1)} %bitcast.21), channel_id=1, source_target_pairs={{0,2},{2,4},{4,6},{6,8},{8,10},{10,12},{12,14},{14,16},{16,18},{18... | collective-permute-start | bytes 4718600 | tf_op jit(solution)/shard_map/ppermute | solution.py:13
  92.5 85.3 %collective-permute-start.1 = (f32[1536,256]{1,0:T(8,128)S(1)}, f32[1536,256]{1,0:T(8,128)S(1)}, u32[]{:S(2)}, u32[]{:S(2)}) collective-permute-start(f32[1536,256]{1,0:T(8,128)S(1)} %bitcast.20), channel_id=1, source_target_pairs={{0,30},{2,0},{4,2},{6,4},{8,6},{10,8},{12,10},{14,12},{16,14},{18,... | collective-permute-start | bytes 4718600 | tf_op jit(solution)/shard_map/ppermute | solution.py:13
  97.0 100.2 %collective-permute-start = (f32[1536,256]{1,0:T(8,128)S(1)}, f32[1536,256]{1,0:T(8,128)S(1)}, u32[]{:S(2)}, u32[]{:S(2)}) collective-permute-start(f32[1536,256]{1,0:T(8,128)S(1)} %bitcast.19), channel_id=1, source_target_pairs={{0,28},{2,30},{4,0},{6,2},{8,4},{10,6},{12,8},{14,10},{16,12},{18,... | collective-permute-start | bytes 4718600 | tf_op jit(solution)/shard_map/ppermute | solution.py:13
  198.8 25.0 %copy-start.2 = (bf16[768,256]{1,0:T(8,128)(2,1)S(1)}, bf16[768,256]{1,0:T(8,128)(2,1)}, u32[]{:S(2)}) copy-start(bf16[768,256]{1,0:T(8,128)(2,1)} %param.9) | copy-start | bytes 1179652
  198.8 157.7 %all-reduce.2.cloned.1.call-start = ((), (), s32[]{:S(2)}) async-start(), calls=%async_computation.2 | async-start | bytes 524288 | tf_op jit(solution)/shard_map/psum | solution.py:35
  223.8 2.3 copy-start.1
Sparse Core Ops, SparseCore 0:
  198.9 24.8 reduce-scatter.1
  229.9 126.5 all-reduce.1
where the time goes:
time: 366 us; the launch traced here: 365 us
  waiting for transfers between devices  254 us (69%)
  other arithmetic  43.1 us (12%)
  local copies, waits for them, and re-layouts  29.9 us (8%)
  matrix products  15.4 us (4%)
  between operations  14.1 us (4%)
  starting transfers between devices  8.1 us (2%)
    psum x1, waiting for transfers between devices, local(): lax.psum(weight_term, ('blk', 'rep')) * (1.0 / math.sqrt(node_count))  129 us
    ppermute x4, waiting for transfers between devices, shifted(): lax.ppermute(value, axis, [(i, (i + by) % devices) for i in range(devices)])  100 us
    scatter-add x1, other arithmetic, local(): jax.ops.segment_sum(tiles, block_cols, num_segments=spans * stripe_blocks)  37.6 us
    reduce_scatter x1, waiting for transfers between devices, local(): mine = lax.psum_scatter(total, 'rep', scatter_dimension=0, tiled=True)  24.9 us
    dot_general x1, local copies, waits for them, and re-layouts, local(): jnp.einsum('kab,kaf->kbf', block_values, picked, preferred_element_type=j...  15.6 us
    dot_general x1, matrix products, local(): jnp.einsum('kab,kaf->kbf', block_values, picked, preferred_element_type=j...  12.1 us
    ppermute x4, starting transfers between devices, shifted(): lax.ppermute(value, axis, [(i, (i + by) % devices) for i in range(devices)])  8.02 us
  transfers between devices with their start and end apart: 6, of which 4 were waited for; matrix products, arithmetic and copies ran while one was open for 0% of the time, Pallas kernels for 0%

commit v1 on v0

v1 whole, which is shorter than its diff:
```python
import functools
import math

import jax
import jax.numpy as jnp
from jax import lax
from jax.experimental import pallas as pl
from jax.experimental.pallas import tpu as pltpu
from jax.sharding import PartitionSpec as P

HALO = 2
SPANS = 2 * HALO + 1
MESH = pl.DeviceIdType.MESH
VMEM_MAX = 67_043_328
CHUNKS = 8
GROUP = 4
STEP = 24


def window_kernel(rows_ref, cols_ref, grad_ref, pre_ref, values_ref, out_ref, masked, window, sem):
    step = pl.program_id(0)

    @pl.when(step == 0)
    def _():
        masked[...] = jnp.where(pre_ref[...] > 0, grad_ref[...], jnp.zeros_like(grad_ref[...])).reshape(masked.shape)

        @pl.loop(0, window.shape[0])
        def _(i):
            window[i] = jnp.zeros(window.shape[1:], window.dtype)

    count = values_ref.shape[0]

    @pl.loop(0, count // GROUP)
    def _(group):
        tiles = []
        for i in range(GROUP):
            k = group * GROUP + i
            tiles.append(
                lax.dot_general(
                    values_ref[k],
                    masked[rows_ref[step * count + k]],
                    (((0,), (0,)), ((), ())),
                    preferred_element_type=jnp.float32,
                )
            )
        for i in range(GROUP):
            col = cols_ref[step * count + group * GROUP + i]
            window[col] = window[col] + tiles[i]

    @pl.when(step == pl.num_programs(0) - 1)
    def _():
        copy = pltpu.make_async_copy(window, out_ref, sem)
        copy.start()
        copy.wait()


def window_sums(rows, cols, grad_out, pre_act, values):
    count, block, _ = values.shape
    stripe_rows, width = grad_out.shape
    stripe_blocks = stripe_rows // block
    whole = pl.BlockSpec((stripe_rows, width), lambda i, *_: (0, 0))
    return pl.pallas_call(
        window_kernel,
        out_shape=jax.ShapeDtypeStruct((SPANS * stripe_blocks, block, width), jnp.float32),
        grid_spec=pltpu.PrefetchScalarGridSpec(
            num_scalar_prefetch=2,
            grid=(count // STEP,),
            in_specs=[whole, whole, pl.BlockSpec((STEP, block, block), lambda i, *_: (i, 0, 0))],
            out_specs=pl.BlockSpec(memory_space=pl.ANY),
            scratch_shapes=[
                pltpu.VMEM((stripe_blocks, block, width), jnp.bfloat16),
                pltpu.VMEM((SPANS * stripe_blocks, block, width), jnp.float32),
                pltpu.SemaphoreType.DMA,
            ],
        ),
        compiler_params=pltpu.CompilerParams(vmem_limit_bytes=56 << 20),
        name="window_sums",
    )(rows, cols, grad_out, pre_act, values)


def exchange_kernel(
    nb, nr, scale,
    win, prev_ref, weight_ref, grad_in_ref, gw_ref,
    acc, core_in, z_in, y_in, x_in, dy, term, term_in, rep_in, total,
    s_load, s_core, r_core, s_z, r_z, s_y, r_y, s_x, r_x, s_t, r_t, s_r, r_r, s_g, r_g,
):
    b, r = lax.axis_index("blk"), lax.axis_index("rep")
    core, chip = b % 2, b // 2
    y, chips = chip % 2, nb // 2
    rows = dy.shape[0]
    size = rows // CHUNKS

    loads = [pltpu.make_async_copy(win.at[2 * i], acc.at[i], s_load.at[i]) for i in range(3)]
    for load in loads:
        load.start()

    barrier = pltpu.get_barrier_semaphore()
    for d in range(1, nb):
        pl.semaphore_signal(barrier, inc=1, device_id=((b + d) % nb, r), device_id_type=MESH)
    for e in range(1, nr):
        pl.semaphore_signal(barrier, inc=1, device_id=(b, (r + e) % nr), device_id_type=MESH)
    pl.semaphore_wait(barrier, nb - 1 + nr - 1)

    def remote(src, dst, send, recv, to_b, to_r):
        return pltpu.make_async_remote_copy(
            src_ref=src, dst_ref=dst, send_sem=send, recv_sem=recv,
            device_id=(to_b, to_r), device_id_type=MESH,
        )

    def part(j):
        return pl.ds(j * size, size)

    far, near = 2 * y, 2 - 2 * y
    core_to = chip * 2 + 1 - core
    z_to = ((chip + 4 * y - 2 + chips) % chips) * 2 + core
    y_to = (chip + 1 - 2 * y) * 2 + core

    def core_copy(i, j):
        return remote(
            win.at[2 * i + 1, :, part(j), :], core_in.at[i, :, part(j), :],
            s_core.at[i, j], r_core.at[i, j], core_to, r,
        )

    def z_copy(j):
        return remote(acc.at[far, :, part(j), :], z_in.at[:, part(j), :], s_z.at[j], r_z.at[j], z_to, r)

    def y_copy(j):
        return remote(acc.at[near, :, part(j), :], y_in.at[:, part(j), :], s_y.at[j], r_y.at[j], y_to, r)

    def x_copy(e, j):
        q = (r + e) % nr
        return remote(acc.at[1, q, part(j), :], x_in.at[e, part(j), :], s_x.at[e, j], r_x.at[e, j], b, q)

    for j in range(CHUNKS):
        for i in range(2):
            core_copy(i, j).start()
    for load in loads:
        load.wait()

    for j in range(CHUNKS):
        for i in range(2):
            core_copy(i, j).wait_recv()
            acc[1 + i - core, :, part(j), :] += core_in[i, :, part(j), :]
        z_copy(j).start()

    for step in range(CHUNKS + 3):
        if step < CHUNKS:
            j = step
            z_copy(j).wait_recv()
            acc[near, :, part(j), :] += z_in[:, part(j), :]
            y_copy(j).start()
        if 0 <= step - 1 < CHUNKS:
            j = step - 1
            y_copy(j).wait_recv()
            acc[1, :, part(j), :] += y_in[:, part(j), :]
            for e in range(1, nr):
                x_copy(e, j).start()
        if 0 <= step - 3 < CHUNKS:
            j = step - 3
            mine = acc[1, r, part(j), :]
            for e in range(1, nr):
                x_copy(e, j).wait_recv()
                mine = mine + x_in[e, part(j), :]
            dy[part(j), :] = mine.astype(jnp.bfloat16)

    prev = prev_ref[...]
    feats = jnp.maximum(prev, jnp.zeros_like(prev))
    product = lax.dot_general(feats, dy[...], (((0,), (0,)), ((), ())), preferred_element_type=jnp.float32)
    term[...] = product.reshape(term.shape)

    def term_copy(d):
        to = (b + d) % nb
        return remote(term.at[to], term_in.at[d], s_t.at[d], r_t.at[d], to, r)

    def rep_copy(e):
        return remote(rep_in.at[r], rep_in.at[r], s_r.at[e], r_r.at[e], b, (r + e) % nr)

    def total_copy(d):
        return remote(total.at[b], total.at[b], s_g.at[d], r_g.at[d], (b + d) % nb, r)

    for d in range(1, nb):
        term_copy(d).start()
    back = lax.dot_general(dy[...], weight_ref[...], (((1,), (1,)), ((), ())), preferred_element_type=jnp.float32)
    grad_in_ref[...] = jnp.where(prev > 0, back, jnp.zeros_like(back)).astype(jnp.bfloat16)
    own = term[b]
    for d in range(1, nb):
        term_copy(d).wait_recv()
        own = own + term_in[d]
    rep_in[r] = own
    for e in range(1, nr):
        rep_copy(e).start()
    for e in range(1, nr):
        rep_copy(e).wait_recv()
    full = rep_in[0]
    for e in range(1, nr):
        full = full + rep_in[e]
    total[b] = full * scale
    for d in range(1, nb):
        total_copy(d).start()
    for d in range(1, nb):
        total_copy(d).wait_recv()
    gw_ref[...] = total[...].reshape(gw_ref.shape)

    for j in range(CHUNKS):
        for i in range(2):
            core_copy(i, j).wait_send()
        z_copy(j).wait_send()
        y_copy(j).wait_send()
        for e in range(1, nr):
            x_copy(e, j).wait_send()
    for d in range(1, nb):
        term_copy(d).wait_send()
        total_copy(d).wait_send()
    for e in range(1, nr):
        rep_copy(e).wait_send()


def exchange(nb, nr, window, prev_pre, weight, nodes):
    rows, width = prev_pre.shape
    slab = (nr, rows, width)
    f32 = jnp.float32
    piece = (width // nb, width)
    need = 4 * width * rows * (7 * nr + nr + 2) + 12 * 4 * width * width
    dma = pltpu.SemaphoreType.DMA
    vmem = pl.BlockSpec(memory_space=pltpu.VMEM)
    return pl.pallas_call(
        functools.partial(exchange_kernel, nb, nr, 1.0 / math.sqrt(nodes)),
        out_shape=(
            jax.ShapeDtypeStruct((rows, width), jnp.bfloat16),
            jax.ShapeDtypeStruct((width, width), f32),
        ),
        in_specs=[pl.BlockSpec(memory_space=pl.ANY), vmem, vmem],
        out_specs=(vmem, vmem),
        scratch_shapes=[
            pltpu.VMEM((3,) + slab, f32),
            pltpu.VMEM((2,) + slab, f32),
            pltpu.VMEM(slab, f32),
            pltpu.VMEM(slab, f32),
            pltpu.VMEM(slab, f32),
            pltpu.VMEM((rows, width), jnp.bfloat16),
            pltpu.VMEM((nb,) + piece, f32),
            pltpu.VMEM((nb,) + piece, f32),
            pltpu.VMEM((nr,) + piece, f32),
            pltpu.VMEM((nb,) + piece, f32),
            dma((3,)),
            dma((2, CHUNKS)), dma((2, CHUNKS)),
            dma((CHUNKS,)), dma((CHUNKS,)),
            dma((CHUNKS,)), dma((CHUNKS,)),
            dma((nr, CHUNKS)), dma((nr, CHUNKS)),
            dma((nb,)), dma((nb,)),
            dma((nr,)), dma((nr,)),
            dma((nb,)), dma((nb,)),
        ],
        compiler_params=pltpu.CompilerParams(
            collective_id=0, has_side_effects=True, vmem_limit_bytes=min(VMEM_MAX, need + (4 << 20))
        ),
        name="exchange",
    )(window, prev_pre, weight)


def local(nb, nr, grad_out, pre_act, prev_pre, weight, block_values, block_rows, block_cols):
    stripe_rows, width = grad_out.shape
    window = window_sums(block_rows, block_cols, grad_out, pre_act, block_values)
    window = window.reshape(SPANS, nr, stripe_rows // nr, width)
    return tuple(exchange(nb, nr, window, prev_pre, weight, stripe_rows * nb))


def solution(mesh):
    in_specs = (
        P("blk", None),
        P("blk", None),
        P(("blk", "rep"), None),
        P(),
        P(("blk", "rep"), None, None),
        P(("blk", "rep")),
        P(("blk", "rep")),
    )
    out_specs = (P(("blk", "rep"), None), P())
    body = functools.partial(local, mesh.shape["blk"], mesh.shape["rep"])
    return jax.shard_map(body, mesh=mesh, in_specs=in_specs, out_specs=out_specs, check_vma=False)
```

time: 366 us -> 89.6 us (0.24)
  waiting for transfers between devices: 254 us -> 0 us
  Pallas kernels: 0 us -> 84.1 us
  other arithmetic: 43.1 us -> 0 us
  local copies, waits for them, and re-layouts: 29.9 us -> 4.68 us
  matrix products: 15.4 us -> 0 us
  between operations: 14.1 us -> 0.69 us
  starting transfers between devices: 8.1 us -> 0 us
    psum x1 -> x0, waiting for transfers between devices: 129 us -> none  [local(): lax.psum(weight_term, ('blk', 'rep')) * (1.0 / math.sqrt(node_count))]
    ppermute x4 -> x0, waiting for transfers between devices: 100 us -> none  [shifted(): lax.ppermute(value, axis, [(i, (i + by) % devices) for i in range(devices)])]
    pallas_call x0 -> x2, Pallas kernels: none -> 84.1 us  [the longest x1 69.9 us: exchange(): pl.pallas_call(functools.partial(exchange_kernel, nb, nr, 1.0 / math.sqrt...]
    scatter-add x1 -> x0, other arithmetic: 37.6 us -> none  [local(): jax.ops.segment_sum(tiles, block_cols, num_segments=spans * stripe_blocks)]
    reduce_scatter x1 -> x0, waiting for transfers between devices: 24.9 us -> none  [local(): mine = lax.psum_scatter(total, 'rep', scatter_dimension=0, tiled=True)]
    dot_general x1 -> x0, local copies, waits for them, and re-layouts: 15.6 us -> none  [local(): jnp.einsum('kab,kaf->kbf', block_values, picked, preferred_element_type=j...]
    dot_general x3 -> x0, matrix products: 15.4 us -> none  [the longest x1 12.1 us: local(): jnp.einsum('kab,kaf->kbf', block_values, picked, preferred_element_type=j...]
    ppermute x4 -> x0, starting transfers between devices: 8.02 us -> none  [shifted(): lax.ppermute(value, axis, [(i, (i + by) % devices) for i in range(devices)])]
  transfers between devices with their start and end apart: 6 -> 0, of which waited for: 4 -> 0; matrix products, arithmetic and copies ran while one was open for 0% -> 0% of each run, Pallas kernels for 0% -> 0%
where the time goes in v1:
time: 89.6 us; the launch traced here: 89.5 us
  Pallas kernels  84.1 us (94%)
  local copies, waits for them, and re-layouts  4.68 us (5%)
    pallas_call x1, Pallas kernels, exchange(): pl.pallas_call(functools.partial(exchange_kernel, nb, nr, 1.0 / math.sqrt...  69.9 us
    pallas_call x1, Pallas kernels, window_sums(): pl.pallas_call(window_kernel, out_shape=jax.ShapeDtypeStruct((SPANS * str...  14.2 us
    unnamed x8, local copies, waits for them, and re-layouts  4.68 us

profile of v1, /device:TPU:0, one launch (start us, length us, event | category | flops | bytes accessed | tf_op | source)
XLA Modules:
  0.0 89.5 jit_solution(5953681876077259892)
XLA Ops:
  0.6 0.0 copy-start.2
  0.6 0.0 copy-start.1
  0.7 14.2 %window_sums.1 = f32[60,128,256]{2,1,0:T(8,128)} custom-call(s32[120]{0:T(128)} %rows_ref.1, s32[120]{0:T(128)} %cols_ref.1, bf16[1536,256]{1,0:T(8,128)(2,1)} %grad_ref.1, bf16[1536,256]{1,0:T(8,128)(2,1)} %pre_ref.1, bf16[120,128,128]{2,1,0:T(8,128)(2,1)} %values_ref.1), custom_call_target="tpu_custom_call" | custom-call | tf_op jit(solution)/shard_map/window_sums/pallas_call | solution.py:62
  14.9 0.0 copy-done.2
  14.9 0.0 copy-done.1
  14.9 0.0 copy-start
  14.9 3.2 %copy-done = f32[60,128,256]{2,1,0:T(8,128)S(1)} copy-done((f32[60,128,256]{2,1,0:T(8,128)S(1)}, f32[60,128,256]{2,1,0:T(8,128)}, u32[]{:S(2)}) %copy-start) | copy-done | bytes 7864344
  18.1 69.9 %exchange.1 = (bf16[768,256]{1,0:T(8,128)(2,1)S(1)}, f32[256,256]{1,0:T(8,128)S(1)}) custom-call(f32[5,2,768,256]{3,2,1,0:T(8,128)S(1)} %bitcast.1, bf16[768,256]{1,0:T(8,128)(2,1)S(1)} %copy-done.1, bf16[256,256]{1,0:T(8,128)(2,1)S(1)} %copy-done.2), custom_call_target="tpu_custom_call" | custom-call | tf_op jit(solution)/shard_map/exchange/pallas_call | solution.py:226
  88.0 0.7 copy.11
  88.8 0.7 copy.12
Async XLA Ops:
  0.6 14.2 %copy-start.2 = (bf16[256,256]{1,0:T(8,128)(2,1)S(1)}, bf16[256,256]{1,0:T(8,128)(2,1)}, u32[]{:S(2)}) copy-start(bf16[256,256]{1,0:T(8,128)(2,1)} %weight_ref.1) | copy-start | bytes 393220
  0.6 14.2 %copy-start.1 = (bf16[768,256]{1,0:T(8,128)(2,1)S(1)}, bf16[768,256]{1,0:T(8,128)(2,1)}, u32[]{:S(2)}) copy-start(bf16[768,256]{1,0:T(8,128)(2,1)} %prev_ref.1) | copy-start | bytes 1179652
  14.9 3.2 %copy-start = (f32[60,128,256]{2,1,0:T(8,128)S(1)}, f32[60,128,256]{2,1,0:T(8,128)}, u32[]{:S(2)}) copy-start(f32[60,128,256]{2,1,0:T(8,128)} %window_sums.1) | copy-start | bytes 23592964

commit v2 on v1

--- a/solution.py
+++ b/solution.py
@@ -12,7 +12,7 @@
 SPANS = 2 * HALO + 1
 MESH = pl.DeviceIdType.MESH
 VMEM_MAX = 67_043_328
-CHUNKS = 8
+CHUNKS = 16
 GROUP = 4
 STEP = 24
 
@@ -143,20 +143,20 @@
             acc[1 + i - core, :, part(j), :] += core_in[i, :, part(j), :]
         z_copy(j).start()
 
-    for step in range(CHUNKS + 3):
+    for step in range(CHUNKS + 5):
         if step < CHUNKS:
             j = step
             z_copy(j).wait_recv()
             acc[near, :, part(j), :] += z_in[:, part(j), :]
             y_copy(j).start()
-        if 0 <= step - 1 < CHUNKS:
-            j = step - 1
+        if 0 <= step - 2 < CHUNKS:
+            j = step - 2
             y_copy(j).wait_recv()
             acc[1, :, part(j), :] += y_in[:, part(j), :]
             for e in range(1, nr):
                 x_copy(e, j).start()
-        if 0 <= step - 3 < CHUNKS:
-            j = step - 3
+        if 0 <= step - 5 < CHUNKS:
+            j = step - 5
             mine = acc[1, r, part(j), :]
             for e in range(1, nr):
                 x_copy(e, j).wait_recv()
@@ -220,7 +220,6 @@
     slab = (nr, rows, width)
     f32 = jnp.float32
     piece = (width // nb, width)
-    need = 4 * width * rows * (7 * nr + nr + 2) + 12 * 4 * width * width
     dma = pltpu.SemaphoreType.DMA
     vmem = pl.BlockSpec(memory_space=pltpu.VMEM)
     return pl.pallas_call(
@@ -252,7 +251,7 @@
             dma((nb,)), dma((nb,)),
         ],
         compiler_params=pltpu.CompilerParams(
-            collective_id=0, has_side_effects=True, vmem_limit_bytes=min(VMEM_MAX, need + (4 << 20))
+            collective_id=0, has_side_effects=True, vmem_limit_bytes=VMEM_MAX
         ),
         name="exchange",
     )(window, prev_pre, weight)

time: 89.6 us -> 87.6 us (0.978)
  local copies, waits for them, and re-layouts: 4.68 us -> 3.44 us
  Pallas kernels: 84.1 us -> 83.2 us
    unnamed x8 -> x2, local copies, waits for them, and re-layouts: 4.68 us -> 3.44 us
where the time goes in v2:
time: 87.6 us; the launch traced here: 87.3 us
  Pallas kernels  83.2 us (95%)
  local copies, waits for them, and re-layouts  3.44 us (4%)
    pallas_call x1, Pallas kernels, exchange(): pl.pallas_call(functools.partial(exchange_kernel, nb, nr, 1.0 / math.sqrt...  69.2 us
    pallas_call x1, Pallas kernels, window_sums(): pl.pallas_call(window_kernel, out_shape=jax.ShapeDtypeStruct((SPANS * str...  14.1 us
    unnamed x2, local copies, waits for them, and re-layouts  3.44 us

profile of v2, /device:TPU:0, one launch (start us, length us, event | category | flops | bytes accessed | tf_op | source)
XLA Modules:
  0.0 87.3 jit_solution(11033238075713759334)
XLA Ops:
  0.6 14.1 %window_sums.1 = f32[60,128,256]{2,1,0:T(8,128)} custom-call(s32[120]{0:T(128)} %rows_ref.1, s32[120]{0:T(128)} %cols_ref.1, bf16[1536,256]{1,0:T(8,128)(2,1)} %grad_ref.1, bf16[1536,256]{1,0:T(8,128)(2,1)} %pre_ref.1, bf16[120,128,128]{2,1,0:T(8,128)(2,1)} %values_ref.1), custom_call_target="tpu_custom_call" | custom-call | tf_op jit(solution)/shard_map/window_sums/pallas_call | solution.py:62
  14.7 69.2 %exchange.1 = (bf16[768,256]{1,0:T(8,128)(2,1)}, f32[256,256]{1,0:T(8,128)}) custom-call(f32[5,2,768,256]{3,2,1,0:T(8,128)} %bitcast.1, bf16[768,256]{1,0:T(8,128)(2,1)} %prev_ref.1, bf16[256,256]{1,0:T(8,128)(2,1)} %weight_ref.1), custom_call_target="tpu_custom_call" | custom-call | tf_op jit(solution)/shard_map/exchange/pallas_call | solution.py:225
  83.9 1.8 %copy.11 = bf16[768,256]{1,0:T(8,128)(2,1)} copy(bf16[768,256]{1,0:T(8,128)(2,1)} %get-tuple-element.4) | data formatting | bytes 786432
  85.7 1.7 %copy.12 = f32[256,256]{1,0:T(8,128)} copy(f32[256,256]{1,0:T(8,128)} %get-tuple-element.5) | data formatting | bytes 524288
